TPU v7x, 1024 devices: a whole 4x8x16 slice. The times are simulated.
1024 devices in a mesh: ctx: 128 (over z, x, core), head: 8 (over y).
Axes of the slice: x: 4, y: 8, z: 16, core: 2. Of those that a mesh axis runs over, the one named last changes fastest.
Arguments:
- queries: bfloat16 [32768, 64, 128], P('ctx', 'head'), may hold values from -16 to 16
- keys: bfloat16 [32768, 8, 128], P(('ctx', 'head')), may hold values from -8 to 8
- values: bfloat16 [32768, 8, 128], P(('ctx', 'head')), may hold values from -6 to 6
- grad_out: bfloat16 [32768, 64, 128], P('ctx', 'head'), may hold values from -6 to 6
- lengths: int32 [128], replicated, may hold values from 1 to 768, 32768 in all
Outputs:
- attended: bfloat16 [32768, 64, 128], P('ctx', 'head')
- d_queries: bfloat16 [32768, 64, 128], P('ctx', 'head')
- d_keys: bfloat16 [32768, 8, 128], P(('ctx', 'head'))
- d_values: bfloat16 [32768, 8, 128], P(('ctx', 'head'))
Inputs may be any that keep to these rules, and one draw needn't show every extreme that they name: `lengths`: the 128 documents fill the window; the longest has exactly 768 tokens.
All inputs are finite; a program needn't handle non-finite values.
Results may differ from a plain program's by a relative error of at most 0.0085.
Values may be sent and summed in bfloat16 or wider, within the bound.
A program may use at most 64 MiB of HBM per device.

v0:
```python
import jax
import jax.numpy as jnp
from jax import lax
from jax.sharding import PartitionSpec as P

BACK = 3


def side_by_side(arrays, axis, split_dim, concat_dim, along):
    ends, at = ([], 0)
    for a in arrays[:-1]:
        at += a.shape[along]
        ends.append(at)
    both = jnp.concatenate(arrays, axis=along)
    return tuple(
        jnp.split(
            lax.all_to_all(both, axis, split_axis=split_dim, concat_axis=concat_dim, tiled=True),
            ends,
            axis=along,
        )
    )


def shifted(block, axis, distance):
    devices = range(lax.axis_size(axis))
    route = [(i - distance, i) for i in devices if i - distance in devices]
    return lax.ppermute(block, axis, route)


def head_pass(query_rows, grad_rows, key_rows, value_rows, allowed):
    inv_root = query_rows.shape[-1] ** (-0.5)
    scores = jnp.dot(query_rows, key_rows.T, preferred_element_type=jnp.float32) * inv_root
    masked = jnp.where(allowed, scores, -jnp.inf)
    top_score = jnp.max(masked, axis=1, keepdims=True)
    log_total = top_score + jnp.log(jnp.sum(jnp.exp(masked - top_score), axis=1, keepdims=True))
    probs = jnp.exp(masked - log_total)
    probs_low = probs.astype(jnp.bfloat16)
    attended = jnp.dot(probs_low, value_rows, preferred_element_type=jnp.float32).astype(
        jnp.bfloat16
    )
    correction = jnp.sum(
        grad_rows.astype(jnp.float32) * attended.astype(jnp.float32), axis=1, keepdims=True
    )
    grad_probs = jnp.dot(grad_rows, value_rows.T, preferred_element_type=jnp.float32)
    grad_scores = (probs * (grad_probs - correction)).astype(jnp.bfloat16)
    grad_values = jnp.dot(probs_low.T, grad_rows, preferred_element_type=jnp.float32)
    grad_query = (
        jnp.dot(grad_scores, key_rows, preferred_element_type=jnp.float32) * inv_root
    ).astype(jnp.bfloat16)
    grad_keys = jnp.dot(grad_scores.T, query_rows, preferred_element_type=jnp.float32) * inv_root
    return (attended, grad_query, grad_keys, grad_values, log_total, correction)


def group_pass(query_group, grad_group, key_rows, value_rows, allowed):

    def one_head(head_inputs):
        return head_pass(head_inputs[0], head_inputs[1], key_rows, value_rows, allowed)

    attended, grad_query, grad_keys, grad_values, log_total, correction = lax.map(
        one_head, (jnp.moveaxis(query_group, 1, 0), jnp.moveaxis(grad_group, 1, 0))
    )
    return (
        jnp.moveaxis(attended, 0, 1),
        jnp.moveaxis(grad_query, 0, 1),
        jnp.sum(grad_keys, axis=0),
        jnp.sum(grad_values, axis=0),
        jnp.moveaxis(log_total[:, :, 0], 0, 1),
        jnp.moveaxis(correction[:, :, 0], 0, 1),
    )


def attend(query_split, grad_split, key_span, value_span, allowed):
    results = [
        group_pass(query_split[:, 0], grad_split[:, 0], key_span[:, 0], value_span[:, 0], allowed)
    ]
    return tuple(
        (jnp.stack([member[slot_index] for member in results], axis=1) for slot_index in range(6))
    )


def on_device(queries, keys, values, grad_out, lengths):
    key_local, value_local = side_by_side((keys, values), "head", 1, 0, 2)
    tok_dev = queries.shape[0]
    groups = key_local.shape[1]
    head_dim = queries.shape[2]
    per_group = queries.shape[1] // groups
    query_split = queries.reshape(tok_dev, groups, per_group, head_dim)
    grad_split = grad_out.reshape(tok_dev, groups, per_group, head_dim)
    shard = lax.axis_index("ctx")
    query_pos = shard * tok_dev + jnp.arange(tok_dev, dtype=jnp.int32)
    starts = jnp.cumsum(lengths) - lengths
    query_start = jnp.max(
        jnp.where(starts[None, :] <= query_pos[:, None], starts[None, :], 0), axis=1
    )
    near_key, near_value = shifted((key_local, value_local), "ctx", 1)
    far_pair = shifted((key_local, value_local, near_key, near_value), "ctx", 2)
    key_span = jnp.concatenate([far_pair[2], far_pair[0], near_key, key_local], axis=0)
    value_span = jnp.concatenate([far_pair[3], far_pair[1], near_value, value_local], axis=0)
    key_pos = (shard - BACK) * tok_dev + jnp.arange((BACK + 1) * tok_dev, dtype=jnp.int32)
    allowed = (key_pos[None, :] >= query_start[:, None]) & (key_pos[None, :] <= query_pos[:, None])
    attended, grad_query, grad_keys, grad_values, log_total, correction = attend(
        query_split, grad_split, key_span, value_span, allowed
    )
    key_blocks = grad_keys.reshape(BACK + 1, tok_dev, groups, head_dim)
    value_blocks = grad_values.reshape(BACK + 1, tok_dev, groups, head_dim)
    far_back = shifted((key_blocks[1], value_blocks[1], key_blocks[0], value_blocks[0]), "ctx", -2)
    near_back = shifted((key_blocks[2] + far_back[2], value_blocks[2] + far_back[3]), "ctx", -1)
    key_total = key_blocks[3] + far_back[0] + near_back[0]
    value_total = value_blocks[3] + far_back[1] + near_back[1]
    d_keys, d_values = side_by_side(
        (key_total.astype(jnp.bfloat16), value_total.astype(jnp.bfloat16)), "head", 0, 1, 2
    )
    return (
        attended.reshape(tok_dev, groups * per_group, head_dim),
        grad_query.reshape(tok_dev, groups * per_group, head_dim),
        d_keys,
        d_values,
    )


def solution(mesh):
    placed = (
        P("ctx", "head", None),
        P(("ctx", "head"), None, None),
        P(("ctx", "head"), None, None),
        P("ctx", "head", None),
        P(),
    )
    return jax.shard_map(
        on_device,
        mesh=mesh,
        in_specs=placed,
        out_specs=(
            P("ctx", "head", None),
            P("ctx", "head", None),
            P(("ctx", "head"), None, None),
            P(("ctx", "head"), None, None),
        ),
        check_vma=False,
    )
```

profile of v0, /device:TPU:199, one launch (start us, length us, event | category | flops | bytes accessed | tf_op | source)
XLA Modules:
  0.0 121.0 jit_solution(364426291718155826)
XLA Ops:
  0.6 0.9 copy.54
  1.5 0.9 copy.55
  2.3 0.7 pad_maximum_fusion
  3.0 6.8 %all-to-all-start = ((bf16[32,8,256]{2,0,1:T(8,128)(2,1)}), bf16[32,8,256]{2,0,1:T(8,128)(2,1)S(1)}, u32[]{:S(2)}, u32[]{:S(2)}) async-start(bf16[32,8,256]{2,0,1:T(8,128)(2,1)} %pad_maximum_fusion), calls=%async_computation | async-start | bytes 262144 | tf_op jit(solution)/shard_map/all_to_all | solution.py:17
  9.9 0.8 copy.57
  11.6 1.3 %copy.56 = bf16[256,8,128]{0,2,1:T(8,128)(2,1)S(1)} copy(bf16[256,8,128]{2,1,0:T(8,128)(2,1)} %param.10) | data formatting | bytes 1048576 | tf_op args[3]
  12.9 1.1 copy.68
  14.0 3.6 %all-to-all-done = bf16[32,8,256]{2,0,1:T(8,128)(2,1)S(1)} async-done(((bf16[32,8,256]{2,0,1:T(8,128)(2,1)}), bf16[32,8,256]{2,0,1:T(8,128)(2,1)S(1)}, u32[]{:S(2)}, u32[]{:S(2)}) %all-to-all-start) | async-done | bytes 131104 | tf_op jit(solution)/shard_map/all_to_all | solution.py:17
  17.6 7.3 %collective-permute-start = (bf16[256,1,128]{2,0,1:T(8,128)(2,1)S(1)}, bf16[256,1,128]{2,0,1:T(8,128)(2,1)S(1)}, u32[]{:S(2)}, u32[]{:S(2)}) collective-permute-start(bf16[256,1,128]{2,0,1:T(8,128)(2,1)S(1)} %get-tuple-element.203), channel_id=1, source_target_pairs={{0,8},{8,16},{16,24},{24,32},{32,40},{40,48},{48,56},{56,64},{64,7... | collective-permute-start | bytes 196616 | tf_op jit(solution)/shard_map/ppermute | solution.py:27
  25.1 3.1 %collective-permute-start.2 = (bf16[256,1,128]{2,0,1:T(8,128)(2,1)S(1)}, bf16[256,1,128]{2,0,1:T(8,128)(2,1)S(1)}, u32[]{:S(2)}, u32[]{:S(2)}) collective-permute-start(bf16[256,1,128]{2,0,1:T(8,128)(2,1)S(1)} %get-tuple-element.203), channel_id=1, source_target_pairs={{0,16},{8,24},{16,32},{24,40},{32,48},{40,56},{48,64},{56,72},{64,... | collective-permute-start | bytes 196616 | tf_op jit(solution)/shard_map/ppermute | solution.py:27
  28.2 2.2 %collective-permute-start.3 = (bf16[256,1,128]{2,0,1:T(8,128)(2,1)S(1)}, bf16[256,1,128]{2,0,1:T(8,128)(2,1)S(1)}, u32[]{:S(2)}, u32[]{:S(2)}) collective-permute-start(bf16[256,1,128]{2,0,1:T(8,128)(2,1)S(1)} %get-tuple-element.202), channel_id=1, source_target_pairs={{0,8},{8,16},{16,24},{24,32},{32,40},{40,48},{48,56},{56,64},{64,7... | collective-permute-start | bytes 196616 | tf_op jit(solution)/shard_map/ppermute | solution.py:27
  30.4 3.1 %collective-permute-start.1 = (bf16[256,1,128]{2,0,1:T(8,128)(2,1)S(1)}, bf16[256,1,128]{2,0,1:T(8,128)(2,1)S(1)}, u32[]{:S(2)}, u32[]{:S(2)}) collective-permute-start(bf16[256,1,128]{2,0,1:T(8,128)(2,1)S(1)} %collective-permute-done), channel_id=1, source_target_pairs={{0,16},{8,24},{16,32},{24,40},{32,48},{40,56},{48,64},{56,72},{64,... | collective-permute-start | bytes 196616 | tf_op jit(solution)/shard_map/ppermute | solution.py:27
  33.6 2.8 %collective-permute-start.5 = (bf16[256,1,128]{2,0,1:T(8,128)(2,1)S(1)}, bf16[256,1,128]{2,0,1:T(8,128)(2,1)S(1)}, u32[]{:S(2)}, u32[]{:S(2)}) collective-permute-start(bf16[256,1,128]{2,0,1:T(8,128)(2,1)S(1)} %get-tuple-element.202), channel_id=1, source_target_pairs={{0,16},{8,24},{16,32},{24,40},{32,48},{40,56},{48,64},{56,72},{64,... | collective-permute-start | bytes 196616 | tf_op jit(solution)/shard_map/ppermute | solution.py:27
  36.4 3.9 %collective-permute-start.4 = (bf16[256,1,128]{2,0,1:T(8,128)(2,1)S(1)}, bf16[256,1,128]{2,0,1:T(8,128)(2,1)S(1)}, u32[]{:S(2)}, u32[]{:S(2)}) collective-permute-start(bf16[256,1,128]{2,0,1:T(8,128)(2,1)S(1)} %collective-permute-done.3), channel_id=1, source_target_pairs={{0,16},{8,24},{16,32},{24,40},{32,48},{40,56},{48,64},{56,72},{64,... | collective-permute-start | bytes 196616 | tf_op jit(solution)/shard_map/ppermute | solution.py:27
  40.4 1.3 %collective-permute-done.4 = bf16[256,1,128]{2,0,1:T(8,128)(2,1)S(1)} collective-permute-done((bf16[256,1,128]{2,0,1:T(8,128)(2,1)S(1)}, bf16[256,1,128]{2,0,1:T(8,128)(2,1)S(1)}, u32[]{:S(2)}, u32[]{:S(2)}) %collective-permute-start.4) | collective-permute-done | bytes 65568 | tf_op jit(solution)/shard_map/ppermute | solution.py:27
  41.7 34.7 %while.17 = (s32[]{:T(128)}, bf16[8,256,128]{1,2,0:T(8,128)(2,1)S(1)}, bf16[8,256,128]{2,1,0:T(8,128)(2,1)S(1)}, f32[8,1024,128]{2,1,0:T(8,128)}, f32[8,1024,128...) while((s32[]{:T(128)}, ...), condition=%wide.region_6.7_spmd.clone, body=%wide.region_2.6_spmd.clone.sunk | while | flops 407207424 | bytes 9522321 | solution.py:59
  43.3 1.1 fusion.71
  44.4 1.2 %fusion.72 = f32[8,1024,128]{2,1,0:T(8,128)} fusion(f32[8,1024,128]{2,1,0:T(8,128)} %get-tuple-element.302, s32[]{:T(128)} %get-tuple-element.298, bf16[8,256,128]{1,2,0:T(8,128)(2,1)S(1)} %get-tuple-element.319, f32[256,1024]{1,0:T(8,128)S(1)} %get-tuple-element.281, f32[256]{0:T(256)S(1)} %log_add_fusion.2), kind=kOutput, calls=%fused_computation.7.clone.1 | convolution fusion | flops 67633152 | bytes 1640448 | tf_op jit(solution)/shard_map/while/body/eval_jaxpr/dot_general | solution.py:46
  47.6 1.2 fusion.71
  48.8 1.3 %fusion.72 = f32[8,1024,128]{2,1,0:T(8,128)} fusion(f32[8,1024,128]{2,1,0:T(8,128)} %get-tuple-element.302, s32[]{:T(128)} %get-tuple-element.298, bf16[8,256,128]{1,2,0:T(8,128)(2,1)S(1)} %get-tuple-element.319, f32[256,1024]{1,0:T(8,128)S(1)} %get-tuple-element.281, f32[256]{0:T(256)S(1)} %log_add_fusion.2), kind=kOutput, calls=%fused_computation.7.clone.1 | convolution fusion | flops 67633152 | bytes 1640448 | tf_op jit(solution)/shard_map/while/body/eval_jaxpr/dot_general | solution.py:46
  52.0 1.2 fusion.71
  53.2 1.2 %fusion.72 = f32[8,1024,128]{2,1,0:T(8,128)} fusion(f32[8,1024,128]{2,1,0:T(8,128)} %get-tuple-element.302, s32[]{:T(128)} %get-tuple-element.298, bf16[8,256,128]{1,2,0:T(8,128)(2,1)S(1)} %get-tuple-element.319, f32[256,1024]{1,0:T(8,128)S(1)} %get-tuple-element.281, f32[256]{0:T(256)S(1)} %log_add_fusion.2), kind=kOutput, calls=%fused_computation.7.clone.1 | convolution fusion | flops 67633152 | bytes 1640448 | tf_op jit(solution)/shard_map/while/body/eval_jaxpr/dot_general | solution.py:46
  56.3 1.2 fusion.71
  57.5 1.2 %fusion.72 = f32[8,1024,128]{2,1,0:T(8,128)} fusion(f32[8,1024,128]{2,1,0:T(8,128)} %get-tuple-element.302, s32[]{:T(128)} %get-tuple-element.298, bf16[8,256,128]{1,2,0:T(8,128)(2,1)S(1)} %get-tuple-element.319, f32[256,1024]{1,0:T(8,128)S(1)} %get-tuple-element.281, f32[256]{0:T(256)S(1)} %log_add_fusion.2), kind=kOutput, calls=%fused_computation.7.clone.1 | convolution fusion | flops 67633152 | bytes 1640448 | tf_op jit(solution)/shard_map/while/body/eval_jaxpr/dot_general | solution.py:46
  60.7 1.2 fusion.71
  61.8 1.2 %fusion.72 = f32[8,1024,128]{2,1,0:T(8,128)} fusion(f32[8,1024,128]{2,1,0:T(8,128)} %get-tuple-element.302, s32[]{:T(128)} %get-tuple-element.298, bf16[8,256,128]{1,2,0:T(8,128)(2,1)S(1)} %get-tuple-element.319, f32[256,1024]{1,0:T(8,128)S(1)} %get-tuple-element.281, f32[256]{0:T(256)S(1)} %log_add_fusion.2), kind=kOutput, calls=%fused_computation.7.clone.1 | convolution fusion | flops 67633152 | bytes 1640448 | tf_op jit(solution)/shard_map/while/body/eval_jaxpr/dot_general | solution.py:46
  65.0 1.2 fusion.71
  66.2 1.3 %fusion.72 = f32[8,1024,128]{2,1,0:T(8,128)} fusion(f32[8,1024,128]{2,1,0:T(8,128)} %get-tuple-element.302, s32[]{:T(128)} %get-tuple-element.298, bf16[8,256,128]{1,2,0:T(8,128)(2,1)S(1)} %get-tuple-element.319, f32[256,1024]{1,0:T(8,128)S(1)} %get-tuple-element.281, f32[256]{0:T(256)S(1)} %log_add_fusion.2), kind=kOutput, calls=%fused_computation.7.clone.1 | convolution fusion | flops 67633152 | bytes 1640448 | tf_op jit(solution)/shard_map/while/body/eval_jaxpr/dot_general | solution.py:46
  69.4 1.1 fusion.71
  70.5 1.2 %fusion.72 = f32[8,1024,128]{2,1,0:T(8,128)} fusion(f32[8,1024,128]{2,1,0:T(8,128)} %get-tuple-element.302, s32[]{:T(128)} %get-tuple-element.298, bf16[8,256,128]{1,2,0:T(8,128)(2,1)S(1)} %get-tuple-element.319, f32[256,1024]{1,0:T(8,128)S(1)} %get-tuple-element.281, f32[256]{0:T(256)S(1)} %log_add_fusion.2), kind=kOutput, calls=%fused_computation.7.clone.1 | convolution fusion | flops 67633152 | bytes 1640448 | tf_op jit(solution)/shard_map/while/body/eval_jaxpr/dot_general | solution.py:46
  73.7 1.2 fusion.71
  74.8 1.2 %fusion.72 = f32[8,1024,128]{2,1,0:T(8,128)} fusion(f32[8,1024,128]{2,1,0:T(8,128)} %get-tuple-element.302, s32[]{:T(128)} %get-tuple-element.298, bf16[8,256,128]{1,2,0:T(8,128)(2,1)S(1)} %get-tuple-element.319, f32[256,1024]{1,0:T(8,128)S(1)} %get-tuple-element.281, f32[256]{0:T(256)S(1)} %log_add_fusion.2), kind=kOutput, calls=%fused_computation.7.clone.1 | convolution fusion | flops 67633152 | bytes 1640448 | tf_op jit(solution)/shard_map/while/body/eval_jaxpr/dot_general | solution.py:46
  76.4 2.4 %reduce_sum.36 = f32[1024,128]{1,0:T(8,128)S(1)} reduce(f32[8,1024,128]{2,1,0:T(8,128)} %get-tuple-element.61, f32[]{:T(128)} %constant.29.clone.1), dimensions={0}, to_apply=%region_7.8 | reduce | flops 917504 | bytes 4718596 | tf_op jit(solution)/shard_map/reduce_sum | solution.py:65
  78.9 2.2 %collective-permute-start.7 = (f32[256,1,128]{2,0,1:T(8,128)S(1)}, f32[256,1,128]{2,0,1:T(8,128)S(1)}, u32[]{:S(2)}, u32[]{:S(2)}) collective-permute-start(f32[256,1,128]{2,0,1:T(8,128)S(1)} %get-tuple-element.197), channel_id=1, source_target_pairs={{16,0},{24,8},{32,16},{40,24},{48,32},{56,40},{64,48},{72,56},{80,... | collective-permute-start | bytes 393224 | tf_op jit(solution)/shard_map/ppermute | solution.py:27
  81.1 2.2 %collective-permute-start.6 = (f32[256,1,128]{2,0,1:T(8,128)S(1)}, f32[256,1,128]{2,0,1:T(8,128)S(1)}, u32[]{:S(2)}, u32[]{:S(2)}) collective-permute-start(f32[256,1,128]{2,0,1:T(8,128)S(1)} %get-tuple-element.196), channel_id=1, source_target_pairs={{16,0},{24,8},{32,16},{40,24},{48,32},{56,40},{64,48},{72,56},{80,... | collective-permute-start | bytes 393224 | tf_op jit(solution)/shard_map/ppermute | solution.py:27
  83.3 2.4 %reduce_sum.37 = f32[1024,128]{1,0:T(8,128)S(1)} reduce(f32[8,1024,128]{2,1,0:T(8,128)} %get-tuple-element.62, f32[]{:T(128)} %constant.29.clone.1), dimensions={0}, to_apply=%region_8.9 | reduce | flops 917504 | bytes 4718596 | tf_op jit(solution)/shard_map/reduce_sum | solution.py:66
  85.8 4.3 %collective-permute-start.10 = (f32[256,1,128]{2,0,1:T(8,128)S(1)}, f32[256,1,128]{2,0,1:T(8,128)S(1)}, u32[]{:S(2)}, u32[]{:S(2)}) collective-permute-start(f32[256,1,128]{2,0,1:T(8,128)S(1)} %get-tuple-element.199), channel_id=1, source_target_pairs={{16,0},{24,8},{32,16},{40,24},{48,32},{56,40},{64,48},{72,56},{80,... | collective-permute-start | bytes 393224 | tf_op jit(solution)/shard_map/ppermute | solution.py:27
  90.0 1.9 %collective-permute-start.9 = (f32[256,1,128]{2,0,1:T(8,128)S(1)}, f32[256,1,128]{2,0,1:T(8,128)S(1)}, u32[]{:S(2)}, u32[]{:S(2)}) collective-permute-start(f32[256,1,128]{2,0,1:T(8,128)S(1)} %get-tuple-element.198), channel_id=1, source_target_pairs={{16,0},{24,8},{32,16},{40,24},{48,32},{56,40},{64,48},{72,56},{80,... | collective-permute-start | bytes 393224 | tf_op jit(solution)/shard_map/ppermute | solution.py:27
  92.0 4.7 %collective-permute-start.8 = (f32[256,1,128]{2,0,1:T(8,128)S(1)}, f32[256,1,128]{2,0,1:T(8,128)S(1)}, u32[]{:S(2)}, u32[]{:S(2)}) collective-permute-start(f32[256,1,128]{2,0,1:T(8,128)S(1)} %fusion.30), channel_id=1, source_target_pairs={{8,0},{16,8},{24,16},{32,24},{40,32},{48,40},{56,48},{64,56},{72,6... | collective-permute-start | bytes 393224 | tf_op jit(solution)/shard_map/ppermute | solution.py:27
  96.7 3.7 %collective-permute-start.11 = (f32[256,1,128]{2,0,1:T(8,128)S(1)}, f32[256,1,128]{2,0,1:T(8,128)S(1)}, u32[]{:S(2)}, u32[]{:S(2)}) collective-permute-start(f32[256,1,128]{2,0,1:T(8,128)S(1)} %fusion.26), channel_id=1, source_target_pairs={{8,0},{16,8},{24,16},{32,24},{40,32},{48,40},{56,48},{64,56},{72,6... | collective-permute-start | bytes 393224 | tf_op jit(solution)/shard_map/ppermute | solution.py:27
  100.4 3.8 %collective-permute-done.8 = f32[256,1,128]{2,0,1:T(8,128)S(1)} collective-permute-done((f32[256,1,128]{2,0,1:T(8,128)S(1)}, f32[256,1,128]{2,0,1:T(8,128)S(1)}, u32[]{:S(2)}, u32[]{:S(2)}) %collective-permute-start.8) | collective-permute-done | bytes 131104 | tf_op jit(solution)/shard_map/ppermute | solution.py:27
  104.3 2.0 %collective-permute-done.11 = f32[256,1,128]{2,0,1:T(8,128)S(1)} collective-permute-done((f32[256,1,128]{2,0,1:T(8,128)S(1)}, f32[256,1,128]{2,0,1:T(8,128)S(1)}, u32[]{:S(2)}, u32[]{:S(2)}) %collective-permute-start.11) | collective-permute-done | bytes 131104 | tf_op jit(solution)/shard_map/ppermute | solution.py:27
  106.9 0.7 reduce.1
  107.6 0.7 reshape.73
  108.3 3.4 %all-to-all-start.1 = ((bf16[8,2,4096]{2,1,0:T(2,128)(2,1)}), bf16[8,2,4096]{2,1,0:T(2,128)(2,1)S(1)}, u32[]{:S(2)}, u32[]{:S(2)}) async-start(bf16[8,2,4096]{2,1,0:T(2,128)(2,1)} %reshape.73), calls=%async_computation.1 | async-start | bytes 262144 | tf_op jit(solution)/shard_map/all_to_all | solution.py:17
  111.6 1.1 copy.59
  112.7 1.1 copy.67
  113.8 5.6 %all-to-all-done.1 = bf16[8,2,4096]{2,1,0:T(2,128)(2,1)S(1)} async-done(((bf16[8,2,4096]{2,1,0:T(2,128)(2,1)}), bf16[8,2,4096]{2,1,0:T(2,128)(2,1)S(1)}, u32[]{:S(2)}, u32[]{:S(2)}) %all-to-all-start.1) | async-done | bytes 131104 | tf_op jit(solution)/shard_map/all_to_all | solution.py:17
  (91 shorter events, 18.5 us)
Async XLA Ops:
  3.0 14.6 %all-to-all-start = ((bf16[32,8,256]{2,0,1:T(8,128)(2,1)}), bf16[32,8,256]{2,0,1:T(8,128)(2,1)S(1)}, u32[]{:S(2)}, u32[]{:S(2)}) async-start(bf16[32,8,256]{2,0,1:T(8,128)(2,1)} %pad_maximum_fusion), calls=%async_computation | async-start | bytes 262144 | tf_op jit(solution)/shard_map/all_to_all | solution.py:17
  17.6 12.8 %collective-permute-start = (bf16[256,1,128]{2,0,1:T(8,128)(2,1)S(1)}, bf16[256,1,128]{2,0,1:T(8,128)(2,1)S(1)}, u32[]{:S(2)}, u32[]{:S(2)}) collective-permute-start(bf16[256,1,128]{2,0,1:T(8,128)(2,1)S(1)} %get-tuple-element.203), channel_id=1, source_target_pairs={{0,8},{8,16},{16,24},{24,32},{32,40},{40,48},{48,56},{56,64},{64,7... | collective-permute-start | bytes 196616 | tf_op jit(solution)/shard_map/ppermute | solution.py:27
  25.1 15.3 %collective-permute-start.2 = (bf16[256,1,128]{2,0,1:T(8,128)(2,1)S(1)}, bf16[256,1,128]{2,0,1:T(8,128)(2,1)S(1)}, u32[]{:S(2)}, u32[]{:S(2)}) collective-permute-start(bf16[256,1,128]{2,0,1:T(8,128)(2,1)S(1)} %get-tuple-element.203), channel_id=1, source_target_pairs={{0,16},{8,24},{16,32},{24,40},{32,48},{40,56},{48,64},{56,72},{64,... | collective-permute-start | bytes 196616 | tf_op jit(solution)/shard_map/ppermute | solution.py:27
  28.2 8.2 %collective-permute-start.3 = (bf16[256,1,128]{2,0,1:T(8,128)(2,1)S(1)}, bf16[256,1,128]{2,0,1:T(8,128)(2,1)S(1)}, u32[]{:S(2)}, u32[]{:S(2)}) collective-permute-start(bf16[256,1,128]{2,0,1:T(8,128)(2,1)S(1)} %get-tuple-element.202), channel_id=1, source_target_pairs={{0,8},{8,16},{16,24},{24,32},{32,40},{40,48},{48,56},{56,64},{64,7... | collective-permute-start | bytes 196616 | tf_op jit(solution)/shard_map/ppermute | solution.py:27
  30.4 9.9 %collective-permute-start.1 = (bf16[256,1,128]{2,0,1:T(8,128)(2,1)S(1)}, bf16[256,1,128]{2,0,1:T(8,128)(2,1)S(1)}, u32[]{:S(2)}, u32[]{:S(2)}) collective-permute-start(bf16[256,1,128]{2,0,1:T(8,128)(2,1)S(1)} %collective-permute-done), channel_id=1, source_target_pairs={{0,16},{8,24},{16,32},{24,40},{32,48},{40,56},{48,64},{56,72},{64,... | collective-permute-start | bytes 196616 | tf_op jit(solution)/shard_map/ppermute | solution.py:27
  33.6 6.8 %collective-permute-start.5 = (bf16[256,1,128]{2,0,1:T(8,128)(2,1)S(1)}, bf16[256,1,128]{2,0,1:T(8,128)(2,1)S(1)}, u32[]{:S(2)}, u32[]{:S(2)}) collective-permute-start(bf16[256,1,128]{2,0,1:T(8,128)(2,1)S(1)} %get-tuple-element.202), channel_id=1, source_target_pairs={{0,16},{8,24},{16,32},{24,40},{32,48},{40,56},{48,64},{56,72},{64,... | collective-permute-start | bytes 196616 | tf_op jit(solution)/shard_map/ppermute | solution.py:27
  36.4 5.2 %collective-permute-start.4 = (bf16[256,1,128]{2,0,1:T(8,128)(2,1)S(1)}, bf16[256,1,128]{2,0,1:T(8,128)(2,1)S(1)}, u32[]{:S(2)}, u32[]{:S(2)}) collective-permute-start(bf16[256,1,128]{2,0,1:T(8,128)(2,1)S(1)} %collective-permute-done.3), channel_id=1, source_target_pairs={{0,16},{8,24},{16,32},{24,40},{32,48},{40,56},{48,64},{56,72},{64,... | collective-permute-start | bytes 196616 | tf_op jit(solution)/shard_map/ppermute | solution.py:27
  78.9 13.1 %collective-permute-start.7 = (f32[256,1,128]{2,0,1:T(8,128)S(1)}, f32[256,1,128]{2,0,1:T(8,128)S(1)}, u32[]{:S(2)}, u32[]{:S(2)}) collective-permute-start(f32[256,1,128]{2,0,1:T(8,128)S(1)} %get-tuple-element.197), channel_id=1, source_target_pairs={{16,0},{24,8},{32,16},{40,24},{48,32},{56,40},{64,48},{72,56},{80,... | collective-permute-start | bytes 393224 | tf_op jit(solution)/shard_map/ppermute | solution.py:27
  81.1 19.3 %collective-permute-start.6 = (f32[256,1,128]{2,0,1:T(8,128)S(1)}, f32[256,1,128]{2,0,1:T(8,128)S(1)}, u32[]{:S(2)}, u32[]{:S(2)}) collective-permute-start(f32[256,1,128]{2,0,1:T(8,128)S(1)} %get-tuple-element.196), channel_id=1, source_target_pairs={{16,0},{24,8},{32,16},{40,24},{48,32},{56,40},{64,48},{72,56},{80,... | collective-permute-start | bytes 393224 | tf_op jit(solution)/shard_map/ppermute | solution.py:27
  85.8 10.9 %collective-permute-start.10 = (f32[256,1,128]{2,0,1:T(8,128)S(1)}, f32[256,1,128]{2,0,1:T(8,128)S(1)}, u32[]{:S(2)}, u32[]{:S(2)}) collective-permute-start(f32[256,1,128]{2,0,1:T(8,128)S(1)} %get-tuple-element.199), channel_id=1, source_target_pairs={{16,0},{24,8},{32,16},{40,24},{48,32},{56,40},{64,48},{72,56},{80,... | collective-permute-start | bytes 393224 | tf_op jit(solution)/shard_map/ppermute | solution.py:27
  90.0 14.3 %collective-permute-start.9 = (f32[256,1,128]{2,0,1:T(8,128)S(1)}, f32[256,1,128]{2,0,1:T(8,128)S(1)}, u32[]{:S(2)}, u32[]{:S(2)}) collective-permute-start(f32[256,1,128]{2,0,1:T(8,128)S(1)} %get-tuple-element.198), channel_id=1, source_target_pairs={{16,0},{24,8},{32,16},{40,24},{48,32},{56,40},{64,48},{72,56},{80,... | collective-permute-start | bytes 393224 | tf_op jit(solution)/shard_map/ppermute | solution.py:27
  92.0 12.3 %collective-permute-start.8 = (f32[256,1,128]{2,0,1:T(8,128)S(1)}, f32[256,1,128]{2,0,1:T(8,128)S(1)}, u32[]{:S(2)}, u32[]{:S(2)}) collective-permute-start(f32[256,1,128]{2,0,1:T(8,128)S(1)} %fusion.30), channel_id=1, source_target_pairs={{8,0},{16,8},{24,16},{32,24},{40,32},{48,40},{56,48},{64,56},{72,6... | collective-permute-start | bytes 393224 | tf_op jit(solution)/shard_map/ppermute | solution.py:27
  96.7 9.6 %collective-permute-start.11 = (f32[256,1,128]{2,0,1:T(8,128)S(1)}, f32[256,1,128]{2,0,1:T(8,128)S(1)}, u32[]{:S(2)}, u32[]{:S(2)}) collective-permute-start(f32[256,1,128]{2,0,1:T(8,128)S(1)} %fusion.26), channel_id=1, source_target_pairs={{8,0},{16,8},{24,16},{32,24},{40,32},{48,40},{56,48},{64,56},{72,6... | collective-permute-start | bytes 393224 | tf_op jit(solution)/shard_map/ppermute | solution.py:27
  108.3 11.2 %all-to-all-start.1 = ((bf16[8,2,4096]{2,1,0:T(2,128)(2,1)}), bf16[8,2,4096]{2,1,0:T(2,128)(2,1)S(1)}, u32[]{:S(2)}, u32[]{:S(2)}) async-start(bf16[8,2,4096]{2,1,0:T(2,128)(2,1)} %reshape.73), calls=%async_computation.1 | async-start | bytes 262144 | tf_op jit(solution)/shard_map/all_to_all | solution.py:17
where the time goes:
time: 122 us; the launch traced here: 121 us
  starting transfers between devices  51.6 us (42%)
  matrix products  31.5 us (26%)
  waiting for transfers between devices  16.3 us (13%)
  other arithmetic  10.4 us (9%)
  local copies, waits for them, and re-layouts  9.82 us (8%)
    ppermute x12, starting transfers between devices, shifted(): return lax.ppermute(block, axis, route)  41.4 us
    all_to_all x2, starting transfers between devices, side_by_side(): lax.all_to_all(both, axis, split_axis=split_dim, concat_axis=concat_dim,...  10.2 us
    dot_general x8, matrix products, head_pass(): jnp.dot(probs_low.T, grad_rows, preferred_element_type=jnp.float32)  9.93 us
    dot_general x8, matrix products, head_pass(): jnp.dot(grad_scores.T, query_rows, preferred_element_type=jnp.float32)  9.29 us
    all_to_all x2, waiting for transfers between devices, side_by_side(): lax.all_to_all(both, axis, split_axis=split_dim, concat_axis=concat_dim,...  9.19 us
    ppermute x12, waiting for transfers between devices, shifted(): return lax.ppermute(block, axis, route)  7.14 us
    unnamed x9, local copies, waits for them, and re-layouts  6.26 us
    dot_general x8, matrix products, head_pass(): jnp.dot(query_rows, key_rows.T, preferred_element_type=jnp.float32)  3.6 us
  transfers between devices with their start and end apart: 14, of which 5 were waited for; matrix products, arithmetic and copies ran while one was open for 8% of the time, Pallas kernels for 0%

commit v1 on v0

v1 whole, which is shorter than its diff:
```python
import functools
import math

import jax
import jax.numpy as jnp
from jax import lax
from jax.experimental import pallas as pl
from jax.experimental.pallas import tpu as pltpu
from jax.sharding import PartitionSpec as P

BACK = 3
SPAN = BACK + 1
TILE = 256
FAR = -1e30
MESH = pl.DeviceIdType.MESH
F32 = jnp.float32
BF16 = jnp.bfloat16
NT = (((1,), (1,)), ((), ()))


def outward(n):
    order = [0]
    for step in range(1, n // 2 + 1):
        order.append(step)
        if n - step != step:
            order.append(n - step)
    return order


def places(n_ctx):
    ctx, head = lax.axis_index("ctx"), lax.axis_index("head")
    core = lax.rem(ctx, 2)

    def at(distance):
        return lax.rem(ctx + n_ctx + distance, n_ctx)

    return head, core, at, at(1 - 2 * core)


def greet(n_head, head, at):
    barrier = pltpu.get_barrier_semaphore()
    for off in range(1, n_head):
        pl.semaphore_signal(
            barrier, inc=1, device_id={"head": lax.rem(head + off, n_head)}, device_id_type=MESH
        )
    for distance in (1, -1, 2, -2):
        pl.semaphore_signal(barrier, inc=1, device_id={"ctx": at(distance)}, device_id_type=MESH)
    return barrier


def remote(src, dst, send, recv, device):
    return pltpu.make_async_remote_copy(
        src_ref=src,
        dst_ref=dst,
        send_sem=send,
        recv_sem=recv,
        device_id=device,
        device_id_type=MESH,
    )


def fused_kernel(
    n_ctx,
    n_head,
    q_hbm,
    k_hbm,
    v_hbm,
    do_hbm,
    len_hbm,
    o_ref,
    dq_ref,
    dk_ref,
    dv_ref,
    qx,
    do_all,
    raw,
    wide,
    len_ref,
    mine,
    span,
    keyx,
    vals,
    keyt,
    valt,
    scores,
    dprob,
    low,
    dsc,
    tops,
    share,
    fix,
    own,
    part,
    land,
    second,
    total,
    home,
    load,
    send,
    recv,
    back_send,
    back_recv,
):
    head, core, at, partner = places(n_ctx)
    shard = lax.axis_index("ctx")
    n_rows, head_dim = do_all.shape
    tok = keyx.shape[0] // SPAN
    per_group = n_rows // tok
    group_rows = tok // n_head
    docs = len_ref.shape[1]
    inv_root = head_dim ** (-0.5)
    expo = inv_root * math.log2(math.e)
    tiles = n_rows // TILE
    order = outward(n_head)
    sends = []

    def started(copy):
        copy.start()
        sends.append(copy)

    barrier = greet(n_head, head, at)
    k_load = pltpu.make_async_copy(k_hbm, raw.at[0], load.at[0])
    v_load = pltpu.make_async_copy(v_hbm, raw.at[1], load.at[1])
    q_load = pltpu.make_async_copy(q_hbm, qx.at[:, pl.ds(0, head_dim)], load.at[2])
    do_load = pltpu.make_async_copy(do_hbm, do_all, load.at[3])
    len_load = pltpu.make_async_copy(len_hbm, len_ref, load.at[4])
    for copy in (k_load, v_load, len_load, q_load, do_load):
        copy.start()
    k_load.wait()
    v_load.wait()
    for which in range(2):
        wide[which] = raw[which].astype(F32)
    for j in range(n_head):
        for which in range(2):
            mine[j, which] = wide[which, pl.ds(j, group_rows, stride=n_head), :].astype(BF16)
    pl.semaphore_wait(barrier, n_head + 3)

    for off in reversed(order[1:]):
        to = lax.rem(head + off, n_head)
        started(
            remote(mine.at[to], span.at[0, head], send.at[0, off], recv.at[0, head], {"head": to})
        )
    started(remote(mine.at[head], span.at[2, head], send.at[2, 0], recv.at[2, head], {"ctx": at(2)}))
    span[0, head] = mine[head]

    len_load.wait()
    counts = len_ref[...].astype(F32)
    row_id = lax.broadcasted_iota(jnp.int32, (docs, docs), 0)
    lane_id = lax.broadcasted_iota(jnp.int32, (docs, docs), 1)
    column = jnp.sum(jnp.where(row_id == lane_id, counts, 0.0), axis=1, keepdims=True)
    ends = jnp.sum(jnp.where(row_id <= lane_id, column, 0.0), axis=0, keepdims=True).astype(jnp.int32)
    starts = ends - len_ref[...]
    for block in range(SPAN):
        pos = (shard - BACK + block) * tok + lax.broadcasted_iota(jnp.int32, (tok, docs), 0)
        inside = (pos >= starts) & (pos < ends)
        keyx[pl.ds(block * tok, tok), pl.ds(head_dim, docs)] = jnp.where(inside, 0.0, FAR).astype(BF16)

    def query_documents(i, carry):
        at_row = pl.ds(pl.multiple_of(i * TILE, TILE), TILE)
        q_tok = i * (TILE // per_group) + lax.broadcasted_iota(jnp.int32, (TILE, docs), 0) // per_group
        pos = shard * tok + q_tok
        inside = (pos >= starts) & (pos < ends)
        qx[at_row, pl.ds(head_dim, docs)] = jnp.where(inside, 1.0, 0.0).astype(BF16)
        return carry

    lax.fori_loop(0, tiles, query_documents, 0)

    for off in order[1:]:
        group = lax.rem(head + off, n_head)
        remote(
            mine.at[0], span.at[0, group], send.at[0, off], recv.at[0, group], {"head": group}
        ).wait_recv()
        started(
            remote(
                span.at[0, group], span.at[2, group], send.at[2, off], recv.at[2, group], {"ctx": at(2)}
            )
        )
    q_load.wait()
    do_load.wait()

    def rows_of(back):
        return pl.ds((BACK - back) * tok, tok)

    def lanes_of(i):
        return pl.ds(pl.multiple_of(i * TILE, TILE), TILE)

    def score_block(back):
        rows = rows_of(back)
        key_rows = span[back, :, 0].reshape(tok, head_dim)
        value_rows = span[back, :, 1].reshape(tok, head_dim)
        keyx[rows, pl.ds(0, head_dim)] = key_rows
        vals[rows, :] = value_rows
        keyt[:, rows] = key_rows.astype(F32).T.astype(BF16)
        valt[:, rows] = value_rows.astype(F32).T.astype(BF16)

        def step(i, carry):
            at_row = lanes_of(i)
            s = lax.dot_general(keyx[rows, :], qx[at_row, :], NT, preferred_element_type=F32)
            if back == 0:
                k_tok = lax.broadcasted_iota(jnp.int32, (tok, TILE), 0)
                r_tok = (
                    i * (TILE // per_group)
                    + lax.broadcasted_iota(jnp.int32, (tok, TILE), 1) // per_group
                )
                s = jnp.where(k_tok <= r_tok, s, FAR)
            scores[rows, at_row] = s
            tops[back : back + 1, at_row] = jnp.max(s, axis=0, keepdims=True)
            dprob[rows, at_row] = lax.dot_general(
                vals[rows, :], do_all[at_row, :], NT, preferred_element_type=F32
            )
            return carry

        lax.fori_loop(0, tiles, step, 0)

    score_block(0)
    for off in order:
        group = lax.rem(head + off, n_head)
        remote(
            span.at[0, group], span.at[2, group], send.at[2, off], recv.at[2, group], {"ctx": at(2)}
        ).wait_recv()
        started(
            remote(
                span.at[2, group], span.at[3, group], send.at[3, off], recv.at[3, group], {"ctx": at(1)}
            )
        )
        started(
            remote(
                span.at[2 * core, group],
                span.at[1, group],
                send.at[1, off],
                recv.at[1, group],
                {"ctx": partner},
            )
        )
    score_block(2)
    for slot, to in ((1, partner), (3, at(1))):
        for off in order:
            group = lax.rem(head + off, n_head)
            remote(
                span.at[2, group], span.at[slot, group], send.at[slot, off], recv.at[slot, group], {"ctx": to}
            ).wait_recv()
        score_block(slot)

    def normalise(i, carry):
        at_row = lanes_of(i)
        top = jnp.max(tops[0:SPAN, at_row], axis=0, keepdims=True) * expo
        mass = jnp.zeros_like(top)
        moment = jnp.zeros_like(top)
        for back in range(SPAN):
            rows = rows_of(back)
            e = jnp.exp2(scores[rows, at_row] * expo - top)
            scores[rows, at_row] = e
            mass = mass + jnp.sum(e, axis=0, keepdims=True)
            moment = moment + jnp.sum(e * dprob[rows, at_row], axis=0, keepdims=True)
        inverse = 1.0 / mass
        share[:, at_row] = inverse
        fix[:, at_row] = moment * inverse
        return carry

    lax.fori_loop(0, tiles, normalise, 0)

    def gradient_block(back):
        rows = rows_of(back)

        def step(i, carry):
            at_row = lanes_of(i)
            p = scores[rows, at_row] * share[:, at_row]
            low[rows, at_row] = p.astype(BF16)
            dsc[rows, at_row] = (p * (dprob[rows, at_row] - fix[:, at_row])).astype(BF16)
            return carry

        lax.fori_loop(0, tiles, step, 0)
        d_k = jnp.dot(dsc[rows, :], qx[:, pl.ds(0, head_dim)], preferred_element_type=F32) * inv_root
        d_v = jnp.dot(low[rows, :], do_all[...], preferred_element_type=F32)
        shape = (n_head, group_rows, head_dim)
        return d_k.reshape(shape), d_v.reshape(shape)

    def settle(back):
        for which, term in enumerate(gradient_block(back)):
            part[back - 1, :, which] = term.astype(BF16)

    for back, slot, to in ((3, 2, at(-1)), (1, 0, partner)):
        settle(back)
        started(remote(part.at[slot], land.at[slot], back_send.at[slot, 0], back_recv.at[slot, 0], {"ctx": to}))
    settle(2)
    for slot, to in ((2, at(-1)), (0, partner)):
        remote(
            part.at[slot], land.at[slot], back_send.at[slot, 0], back_recv.at[slot, 0], {"ctx": to}
        ).wait_recv()
    on_second = (core == 1).astype(F32)
    home_order = order[::-1]
    for off in home_order:
        group = lax.rem(head + off, n_head)
        term = part[1, group].astype(F32) + land[2, group].astype(F32)
        second[group] = (term + on_second * land[0, group].astype(F32)).astype(BF16)
        started(
            remote(
                second.at[group], land.at[1, group], back_send.at[1, off], back_recv.at[1, group], {"ctx": at(-2)}
            )
        )
    for which, term in enumerate(gradient_block(0)):
        own[:, which] = term

    def attended(i, carry):
        at_row = lanes_of(i)
        out = jnp.dot(valt[...], low[:, at_row], preferred_element_type=F32)
        o_ref[at_row, :] = out.T.astype(BF16)
        return carry

    lax.fori_loop(0, tiles, attended, 0)
    for off in home_order:
        group = lax.rem(head + off, n_head)
        remote(
            second.at[group], land.at[1, group], back_send.at[1, off], back_recv.at[1, group], {"ctx": at(-2)}
        ).wait_recv()
        term = own[group] + land[1, group].astype(F32)
        term = (term + (1.0 - on_second) * land[0, group].astype(F32)).astype(BF16)
        if off:
            total[group] = term
            started(
                remote(
                    total.at[group], home.at[head], back_send.at[3, off], back_recv.at[3, head], {"head": group}
                )
            )
        else:
            home[group] = term

    def d_queries(i, carry):
        at_row = lanes_of(i)
        out = jnp.dot(keyt[...], dsc[:, at_row], preferred_element_type=F32) * inv_root
        dq_ref[at_row, :] = out.T.astype(BF16)
        return carry

    lax.fori_loop(0, tiles, d_queries, 0)
    for off in home_order[:-1]:
        group = lax.rem(head + off, n_head)
        remote(
            total.at[group], home.at[group], back_send.at[3, off], back_recv.at[3, group], {"head": group}
        ).wait_recv()
    for j in range(n_head):
        for which in range(2):
            wide[which, pl.ds(j, group_rows, stride=n_head), :] = home[j, which].astype(F32)
    dk_ref[...] = wide[0].astype(BF16)
    dv_ref[...] = wide[1].astype(BF16)
    for copy in sends:
        copy.wait_send()


def store_kernel(*refs):
    count = (len(refs) - 1) // 2
    copies = [
        pltpu.make_async_copy(refs[i], refs[count + i], refs[-1].at[i]) for i in range(count)
    ]
    for copy in copies:
        copy.start()
    for copy in copies:
        copy.wait()


def on_device(n_ctx, n_head, queries, keys, values, grad_out, lengths):
    tok, per_group, head_dim = queries.shape
    group = keys.shape[0]
    rows = tok * per_group
    docs = lengths.shape[0]
    vmem = pl.BlockSpec(memory_space=pltpu.VMEM)
    far = pl.BlockSpec(memory_space=pltpu.HBM)
    share = (n_head, 2, group, head_dim)
    dma = pltpu.SemaphoreType.DMA
    results = (jax.ShapeDtypeStruct((rows, head_dim), BF16),) * 2 + (
        jax.ShapeDtypeStruct((group * n_head, head_dim), BF16),
    ) * 2
    kept = pl.pallas_call(
        functools.partial(fused_kernel, n_ctx, n_head),
        out_shape=results,
        in_specs=[far] * 5,
        out_specs=(vmem,) * 4,
        scratch_shapes=[
            pltpu.VMEM((rows, head_dim + docs), BF16),
            pltpu.VMEM((rows, head_dim), BF16),
            pltpu.VMEM((2, group * n_head, head_dim), BF16),
            pltpu.VMEM((2, group * n_head, head_dim), F32),
            pltpu.VMEM((1, docs), jnp.int32),
            pltpu.VMEM(share, BF16),
            pltpu.VMEM((SPAN,) + share, BF16),
            pltpu.VMEM((SPAN * tok, head_dim + docs), BF16),
            pltpu.VMEM((SPAN * tok, head_dim), BF16),
            pltpu.VMEM((head_dim, SPAN * tok), BF16),
            pltpu.VMEM((head_dim, SPAN * tok), BF16),
            pltpu.VMEM((SPAN * tok, rows), F32),
            pltpu.VMEM((SPAN * tok, rows), F32),
            pltpu.VMEM((SPAN * tok, rows), BF16),
            pltpu.VMEM((SPAN * tok, rows), BF16),
            pltpu.VMEM((8, rows), F32),
            pltpu.VMEM((1, rows), F32),
            pltpu.VMEM((1, rows), F32),
            pltpu.VMEM(share, F32),
            pltpu.VMEM((BACK,) + share, BF16),
            pltpu.VMEM((BACK,) + share, BF16),
            pltpu.VMEM(share, BF16),
            pltpu.VMEM(share, BF16),
            pltpu.VMEM(share, BF16),
            dma((5,)),
            dma((4, n_head)),
            dma((4, n_head)),
            dma((4, n_head)),
            dma((4, n_head)),
        ],
        compiler_params=pltpu.CompilerParams(
            collective_id=0, has_side_effects=True, vmem_limit_bytes=48 << 20
        ),
    )(
        *(
            pltpu.with_memory_space_constraint(x, pltpu.HBM)
            for x in (
                queries.reshape(rows, head_dim),
                keys.reshape(-1, head_dim),
                values.reshape(-1, head_dim),
                grad_out.reshape(rows, head_dim),
                lengths.reshape(1, -1),
            )
        )
    )
    attended, d_queries, d_keys, d_values = pl.pallas_call(
        store_kernel,
        out_shape=results,
        in_specs=[vmem] * 4,
        out_specs=(far,) * 4,
        scratch_shapes=[dma((4,))],
        compiler_params=pltpu.CompilerParams(vmem_limit_bytes=4 << 20),
    )(*kept)
    return (
        attended.reshape(queries.shape),
        d_queries.reshape(queries.shape),
        d_keys.reshape(keys.shape),
        d_values.reshape(values.shape),
    )


def solution(mesh):
    rows, groups = P("ctx", "head", None), P(("ctx", "head"), None, None)
    return jax.shard_map(
        functools.partial(on_device, mesh.shape["ctx"], mesh.shape["head"]),
        mesh=mesh,
        in_specs=(rows, groups, groups, rows, P()),
        out_specs=(rows, rows, groups, groups),
        check_vma=False,
    )
```

time: 122 us -> 58.4 us (0.48)
  the two profiles are of different devices: /device:TPU:199 before, /device:TPU:1 now
where the time goes in v1:
time: 58.4 us; the launch traced here: 58.3 us
  Pallas kernels  57.6 us (99%)
  between operations  0.64 us (1%)
    pallas_call x1, Pallas kernels, on_device(): pl.pallas_call(functools.partial(fused_kernel, n_ctx, n_head), out_shape=...  56.6 us

profile of v1, /device:TPU:1, one launch (start us, length us, event | category | flops | bytes accessed | tf_op | source)
XLA Modules:
  0.0 58.3 jit_solution(17895902893607422577)
XLA Ops:
  0.6 56.6 %shard_map.84 = (bf16[2048,128]{1,0:T(8,128)(2,1)S(1)}, bf16[2048,128]{1,0:T(8,128)(2,1)S(1)}, bf16[256,128]{1,0:T(8,128)(2,1)S(1)}, bf16[256,128]{1,0:T(8,128)(2,1)S(1)}) custom-call(bf16[2048,128]{1,0:T(8,128)(2,1)} %bitcast.9, bf16[256,128]{1,0:T(8,128)(2,1)} %bitcast.11, bf16[256,128]{1,0:T(8,128)(2,1)} %bitcast.12, bf16[2048,128]{1,0:T(8,128)(2,1)} %bitcast.10, ...), custom_call_target="tpu_custom_call" | custom-call | tf_op jit(solution)/shard_map/pallas_call | solution.py:372
  57.2 1.0 %shard_map.85 = (bf16[2048,128]{1,0:T(8,128)(2,1)}, bf16[2048,128]{1,0:T(8,128)(2,1)}, bf16[256,128]{1,0:T(8,128)(2,1)}, bf16[256,128]{1,0:T(8,128)(2,1)}) custom-call(bf16[2048,128]{1,0:T(8,128)(2,1)S(1)} %get-tuple-element.12.refs_0_, bf16[2048,128]{1,0:T(8,128)(2,1)S(1)} %get-tuple-element.13.refs_1_, bf16[256,128]{1,0:T(8,128)(2,1)S(1)} %get-tuple-element.14.refs_2_, ...), custom_call_target="tpu_custom_call" | custom-call | tf_op jit(solution)/shard_map/pallas_call | solution.py:423

commit v2 on v1

--- a/solution.py
+++ b/solution.py
@@ -10,6 +10,8 @@
 
 BACK = 3
 SPAN = BACK + 1
+LAG = 3
+UNROLL = 8
 TILE = 256
 FAR = -1e30
 MESH = pl.DeviceIdType.MESH
@@ -32,20 +34,37 @@
     core = lax.rem(ctx, 2)
 
     def at(distance):
-        return lax.rem(ctx + n_ctx + distance, n_ctx)
-
-    return head, core, at, at(1 - 2 * core)
-
-
-def greet(n_head, head, at):
+        return jnp.clip(ctx + distance, 0, n_ctx - 1)
+
+    return head, core, at, ctx + 1 - 2 * core
+
+
+def is_first(ctx, head):
+    return (ctx == 0) & (head == 0)
+
+
+def greet(n_ctx, n_head, head, shard):
     barrier = pltpu.get_barrier_semaphore()
+    count = jnp.int32(0)
+    greets = jnp.logical_not(is_first(shard, head))
     for off in range(1, n_head):
-        pl.semaphore_signal(
-            barrier, inc=1, device_id={"head": lax.rem(head + off, n_head)}, device_id_type=MESH
-        )
+        to = lax.rem(head + off, n_head)
+
+        @pl.when(greets)
+        def _():
+            pl.semaphore_signal(barrier, inc=1, device_id={"head": to}, device_id_type=MESH)
+
+        count = count + jnp.logical_not(is_first(shard, to)).astype(jnp.int32)
     for distance in (1, -1, 2, -2):
-        pl.semaphore_signal(barrier, inc=1, device_id={"ctx": at(distance)}, device_id_type=MESH)
-    return barrier
+        there = shard + distance
+        exists = (there >= 0) & (there < n_ctx)
+
+        @pl.when(exists & greets)
+        def _():
+            pl.semaphore_signal(barrier, inc=1, device_id={"ctx": there}, device_id_type=MESH)
+
+        count = count + (exists & jnp.logical_not(is_first(there, head))).astype(jnp.int32)
+    return barrier, count
 
 
 def remote(src, dst, send, recv, device):
@@ -100,6 +119,7 @@
     recv,
     back_send,
     back_recv,
+    ready,
 ):
     head, core, at, partner = places(n_ctx)
     shard = lax.axis_index("ctx")
@@ -112,13 +132,29 @@
     expo = inv_root * math.log2(math.e)
     tiles = n_rows // TILE
     order = outward(n_head)
+    near = [lax.rem(head + off, n_head) for off in order]
+    spot = sum(place * (group == 0).astype(jnp.int32) for place, group in enumerate(near))
+    groups = [jnp.where(place < spot, near[place], near[place + 1]) for place in range(n_head - 1)]
+    groups.append(jnp.int32(0))
     sends = []
-
-    def started(copy):
-        copy.start()
-        sends.append(copy)
-
-    barrier = greet(n_head, head, at)
+    always = None
+
+    def started(copy, when=always):
+        if when is None:
+            copy.start()
+        else:
+            pl.when(when)(copy.start)
+        sends.append((copy, when))
+
+    def awaited(copy, when=always):
+        if when is None:
+            copy.wait_recv()
+        else:
+            pl.when(when)(copy.wait_recv)
+
+    back_one, back_two, back_three = shard >= 1, shard >= 2, shard >= 3
+    on_one, on_two = shard + 1 < n_ctx, shard + 2 < n_ctx
+    barrier, greeted = greet(n_ctx, n_head, head, shard)
     k_load = pltpu.make_async_copy(k_hbm, raw.at[0], load.at[0])
     v_load = pltpu.make_async_copy(v_hbm, raw.at[1], load.at[1])
     q_load = pltpu.make_async_copy(q_hbm, qx.at[:, pl.ds(0, head_dim)], load.at[2])
@@ -133,15 +169,43 @@
     for j in range(n_head):
         for which in range(2):
             mine[j, which] = wide[which, pl.ds(j, group_rows, stride=n_head), :].astype(BF16)
-    pl.semaphore_wait(barrier, n_head + 3)
+    pl.semaphore_wait(barrier, greeted)
+
+    @pl.when(is_first(shard, head))
+    def _():
+        for off in range(1, n_head):
+            pl.semaphore_signal(
+                ready, inc=1, device_id={"head": lax.rem(head + off, n_head)}, device_id_type=MESH
+            )
+        for distance in (1, 2):
+            pl.semaphore_signal(ready, inc=1, device_id={"ctx": at(distance)}, device_id_type=MESH)
+
 
     for off in reversed(order[1:]):
         to = lax.rem(head + off, n_head)
         started(
-            remote(mine.at[to], span.at[0, head], send.at[0, off], recv.at[0, head], {"head": to})
-        )
-    started(remote(mine.at[head], span.at[2, head], send.at[2, 0], recv.at[2, head], {"ctx": at(2)}))
+            remote(mine.at[to], span.at[0, head], send.at[0, off], recv.at[0, head], {"head": to}),
+            jnp.logical_not(is_first(shard, to)),
+        )
+    started(
+        remote(mine.at[head], span.at[2, head], send.at[2, head], recv.at[2, head], {"ctx": at(2)}), on_two
+    )
     span[0, head] = mine[head]
+    for slot, there in ((1, back_one), (2, back_two), (3, back_three)):
+
+        @pl.when(jnp.logical_not(there))
+        def _():
+            span[slot] = jnp.zeros(span.shape[1:], BF16)
+
+    for slot, missing in (
+        (0, (core == 1) & (shard < 2)),
+        (1, shard + 2 >= n_ctx),
+        (2, (shard + 1 >= n_ctx) | (shard < 2)),
+    ):
+
+        @pl.when(missing)
+        def _():
+            land[slot] = jnp.zeros(land.shape[1:], BF16)
 
     len_load.wait()
     counts = len_ref[...].astype(F32)
@@ -165,16 +229,61 @@
 
     lax.fori_loop(0, tiles, query_documents, 0)
 
-    for off in order[1:]:
-        group = lax.rem(head + off, n_head)
-        remote(
-            mine.at[0], span.at[0, group], send.at[0, off], recv.at[0, group], {"head": group}
-        ).wait_recv()
+    def relay(group):
+        awaited(
+            remote(
+                span.at[0, group], span.at[2, group], send.at[2, group], recv.at[2, group], {"ctx": at(2)}
+            ),
+            back_two,
+        )
         started(
             remote(
-                span.at[0, group], span.at[2, group], send.at[2, off], recv.at[2, group], {"ctx": at(2)}
-            )
-        )
+                span.at[2, group], span.at[3, group], send.at[3, group], recv.at[3, group], {"ctx": at(1)}
+            ),
+            back_two & on_one,
+        )
+        started(
+            remote(
+                span.at[2 * core, group],
+                span.at[1, group],
+                send.at[1, group],
+                recv.at[1, group],
+                {"ctx": partner},
+            ),
+            (core == 0) | back_two,
+        )
+
+    for place, group in enumerate(groups):
+        other = group != head
+        if place == n_head - 1:
+            follows_first = (shard == 0) & (head > 0)
+
+            @pl.when(follows_first)
+            def _():
+                pl.semaphore_wait(ready, 1)
+
+            started(
+                remote(
+                    mine.at[0],
+                    span.at[0, head],
+                    send.at[0, lax.rem(n_head - head, n_head)],
+                    recv.at[0, head],
+                    {"head": 0},
+                ),
+                follows_first,
+            )
+        awaited(
+            remote(mine.at[0], span.at[0, group], send.at[0, 0], recv.at[0, group], {"head": group}),
+            other,
+        )
+        started(
+            remote(
+                span.at[0, group], span.at[2, group], send.at[2, group], recv.at[2, group], {"ctx": at(2)}
+            ),
+            on_two & other,
+        )
+        if place >= LAG:
+            relay(groups[place - LAG])
     q_load.wait()
     do_load.wait()
 
@@ -195,7 +304,7 @@
 
         def step(i, carry):
             at_row = lanes_of(i)
-            s = lax.dot_general(keyx[rows, :], qx[at_row, :], NT, preferred_element_type=F32)
+            s = lax.dot_general(keyx[rows, :], qx[at_row, :], NT, preferred_element_type=F32) * expo
             if back == 0:
                 k_tok = lax.broadcasted_iota(jnp.int32, (tok, TILE), 0)
                 r_tok = (
@@ -210,45 +319,34 @@
             )
             return carry
 
-        lax.fori_loop(0, tiles, step, 0)
+        lax.fori_loop(0, tiles, step, 0, unroll=UNROLL)
 
     score_block(0)
-    for off in order:
-        group = lax.rem(head + off, n_head)
-        remote(
-            span.at[0, group], span.at[2, group], send.at[2, off], recv.at[2, group], {"ctx": at(2)}
-        ).wait_recv()
-        started(
-            remote(
-                span.at[2, group], span.at[3, group], send.at[3, off], recv.at[3, group], {"ctx": at(1)}
-            )
-        )
-        started(
-            remote(
-                span.at[2 * core, group],
-                span.at[1, group],
-                send.at[1, off],
-                recv.at[1, group],
-                {"ctx": partner},
-            )
-        )
+    for group in groups[n_head - LAG :]:
+        relay(group)
     score_block(2)
-    for slot, to in ((1, partner), (3, at(1))):
-        for off in order:
-            group = lax.rem(head + off, n_head)
-            remote(
-                span.at[2, group], span.at[slot, group], send.at[slot, off], recv.at[slot, group], {"ctx": to}
-            ).wait_recv()
+    for slot, to, there in ((1, partner, back_one), (3, at(1), back_three)):
+        for group in groups:
+            awaited(
+                remote(
+                    span.at[2, group],
+                    span.at[slot, group],
+                    send.at[slot, group],
+                    recv.at[slot, group],
+                    {"ctx": to},
+                ),
+                there,
+            )
         score_block(slot)
 
     def normalise(i, carry):
         at_row = lanes_of(i)
-        top = jnp.max(tops[0:SPAN, at_row], axis=0, keepdims=True) * expo
+        top = jnp.max(tops[0:SPAN, at_row], axis=0, keepdims=True)
         mass = jnp.zeros_like(top)
         moment = jnp.zeros_like(top)
         for back in range(SPAN):
             rows = rows_of(back)
-            e = jnp.exp2(scores[rows, at_row] * expo - top)
+            e = jnp.exp2(scores[rows, at_row] - top)
             scores[rows, at_row] = e
             mass = mass + jnp.sum(e, axis=0, keepdims=True)
             moment = moment + jnp.sum(e * dprob[rows, at_row], axis=0, keepdims=True)
@@ -279,14 +377,31 @@
         for which, term in enumerate(gradient_block(back)):
             part[back - 1, :, which] = term.astype(BF16)
 
-    for back, slot, to in ((3, 2, at(-1)), (1, 0, partner)):
+    @pl.when((head == 0) & ((shard == 1) | (shard == 2)))
+    def _():
+        pl.semaphore_wait(ready, 1)
+
+    far_there = back_two & on_one
+    near_there = (core == 0) | back_two
+    for back, slot, to, there in (
+        (3, 2, at(-1), back_three),
+        (1, 0, partner, (core == 1) | back_two),
+    ):
         settle(back)
-        started(remote(part.at[slot], land.at[slot], back_send.at[slot, 0], back_recv.at[slot, 0], {"ctx": to}))
+        started(
+            remote(
+                part.at[slot], land.at[slot], back_send.at[slot, 0], back_recv.at[slot, 0], {"ctx": to}
+            ),
+            there,
+        )
     settle(2)
-    for slot, to in ((2, at(-1)), (0, partner)):
-        remote(
-            part.at[slot], land.at[slot], back_send.at[slot, 0], back_recv.at[slot, 0], {"ctx": to}
-        ).wait_recv()
+    for slot, to, there in ((2, at(-1), far_there), (0, partner, near_there)):
+        awaited(
+            remote(
+                part.at[slot], land.at[slot], back_send.at[slot, 0], back_recv.at[slot, 0], {"ctx": to}
+            ),
+            there,
+        )
     on_second = (core == 1).astype(F32)
     home_order = order[::-1]
     for off in home_order:
@@ -296,7 +411,8 @@
         started(
             remote(
                 second.at[group], land.at[1, group], back_send.at[1, off], back_recv.at[1, group], {"ctx": at(-2)}
-            )
+            ),
+            back_two,
         )
     for which, term in enumerate(gradient_block(0)):
         own[:, which] = term
@@ -310,9 +426,12 @@
     lax.fori_loop(0, tiles, attended, 0)
     for off in home_order:
         group = lax.rem(head + off, n_head)
-        remote(
-            second.at[group], land.at[1, group], back_send.at[1, off], back_recv.at[1, group], {"ctx": at(-2)}
-        ).wait_recv()
+        awaited(
+            remote(
+                second.at[group], land.at[1, group], back_send.at[1, off], back_recv.at[1, group], {"ctx": at(-2)}
+            ),
+            on_two,
+        )
         term = own[group] + land[1, group].astype(F32)
         term = (term + (1.0 - on_second) * land[0, group].astype(F32)).astype(BF16)
         if off:
@@ -332,18 +451,23 @@
         return carry
 
     lax.fori_loop(0, tiles, d_queries, 0)
-    for off in home_order[:-1]:
+    for off in order:
         group = lax.rem(head + off, n_head)
-        remote(
-            total.at[group], home.at[group], back_send.at[3, off], back_recv.at[3, group], {"head": group}
-        ).wait_recv()
-    for j in range(n_head):
+        if off:
+            awaited(
+                remote(
+                    total.at[group], home.at[group], back_send.at[3, off], back_recv.at[3, group], {"head": group}
+                )
+            )
         for which in range(2):
-            wide[which, pl.ds(j, group_rows, stride=n_head), :] = home[j, which].astype(F32)
+            wide[which, pl.ds(group, group_rows, stride=n_head), :] = home[group, which].astype(F32)
     dk_ref[...] = wide[0].astype(BF16)
     dv_ref[...] = wide[1].astype(BF16)
-    for copy in sends:
-        copy.wait_send()
+    for copy, when in sends:
+        if when is None:
+            copy.wait_send()
+        else:
+            pl.when(when)(copy.wait_send)
 
 
 def store_kernel(*refs):
@@ -404,6 +528,7 @@
             dma((4, n_head)),
             dma((4, n_head)),
             dma((4, n_head)),
+            pltpu.SemaphoreType.REGULAR,
         ],
         compiler_params=pltpu.CompilerParams(
             collective_id=0, has_side_effects=True, vmem_limit_bytes=48 << 20

time: 58.4 us -> 44.6 us (0.76)
  Pallas kernels: 57.6 us -> 43.8 us
    pallas_call x1, Pallas kernels: 56.6 us -> 42.8 us  [on_device(): pl.pallas_call(functools.partial(fused_kernel, n_ctx, n_head), out_shape=...]
where the time goes in v2:
time: 44.6 us; the launch traced here: 44.4 us
  Pallas kernels  43.8 us (98%)
  between operations  0.64 us (1%)
    pallas_call x1, Pallas kernels, on_device(): pl.pallas_call(functools.partial(fused_kernel, n_ctx, n_head), out_shape=...  42.8 us
    pallas_call x1, Pallas kernels, on_device(): pl.pallas_call(store_kernel, out_shape=results, in_specs=[vmem] * 4, out_...  1.03 us

profile of v2, /device:TPU:1, one launch (start us, length us, event | category | flops | bytes accessed | tf_op | source)
XLA Modules:
  0.0 44.4 jit_solution(15292641567309797274)
XLA Ops:
  0.6 42.8 %shard_map.84 = (bf16[2048,128]{1,0:T(8,128)(2,1)S(1)}, bf16[2048,128]{1,0:T(8,128)(2,1)S(1)}, bf16[256,128]{1,0:T(8,128)(2,1)S(1)}, bf16[256,128]{1,0:T(8,128)(2,1)S(1)}) custom-call(bf16[2048,128]{1,0:T(8,128)(2,1)} %bitcast.9, bf16[256,128]{1,0:T(8,128)(2,1)} %bitcast.11, bf16[256,128]{1,0:T(8,128)(2,1)} %bitcast.12, bf16[2048,128]{1,0:T(8,128)(2,1)} %bitcast.10, ...), custom_call_target="tpu_custom_call" | custom-call | tf_op jit(solution)/shard_map/pallas_call | solution.py:496
  43.4 1.0 %shard_map.85 = (bf16[2048,128]{1,0:T(8,128)(2,1)}, bf16[2048,128]{1,0:T(8,128)(2,1)}, bf16[256,128]{1,0:T(8,128)(2,1)}, bf16[256,128]{1,0:T(8,128)(2,1)}) custom-call(bf16[2048,128]{1,0:T(8,128)(2,1)S(1)} %get-tuple-element.12.refs_0_, bf16[2048,128]{1,0:T(8,128)(2,1)S(1)} %get-tuple-element.13.refs_1_, bf16[256,128]{1,0:T(8,128)(2,1)S(1)} %get-tuple-element.14.refs_2_, ...), custom_call_target="tpu_custom_call" | custom-call | tf_op jit(solution)/shard_map/pallas_call | solution.py:548

commit v3 on v2

--- a/solution.py
+++ b/solution.py
@@ -11,7 +11,7 @@
 BACK = 3
 SPAN = BACK + 1
 LAG = 3
-UNROLL = 8
+UNROLL = 4
 TILE = 256
 FAR = -1e30
 MESH = pl.DeviceIdType.MESH
@@ -229,6 +229,16 @@
 
     lax.fori_loop(0, tiles, query_documents, 0)
 
+    def clear(i, carry):
+        at_row = pl.ds(pl.multiple_of(i * TILE, TILE), TILE)
+        for block in (0, BACK):
+            keys = pl.ds(block * tok, tok)
+            low[keys, at_row] = jnp.zeros((tok, TILE), BF16)
+            dsc[keys, at_row] = jnp.zeros((tok, TILE), BF16)
+        return carry
+
+    lax.fori_loop(0, tiles, clear, 0)
+
     def relay(group):
         awaited(
             remote(
@@ -290,6 +300,12 @@
     def rows_of(back):
         return pl.ds((BACK - back) * tok, tok)
 
+    def needed(back, i):
+        base, step = (BACK - back) * tok, TILE // per_group
+        low_key = i * step if back == BACK else 0
+        high_key = (i + 1) * step if back == 0 else tok
+        return pl.ds(base + low_key, high_key - low_key)
+
     def lanes_of(i):
         return pl.ds(pl.multiple_of(i * TILE, TILE), TILE)
 
@@ -302,24 +318,21 @@
         keyt[:, rows] = key_rows.astype(F32).T.astype(BF16)
         valt[:, rows] = value_rows.astype(F32).T.astype(BF16)
 
-        def step(i, carry):
-            at_row = lanes_of(i)
-            s = lax.dot_general(keyx[rows, :], qx[at_row, :], NT, preferred_element_type=F32) * expo
+        for i in range(tiles):
+            at_row = pl.ds(i * TILE, TILE)
+            keys = needed(back, i)
+            s = lax.dot_general(keyx[keys, :], qx[at_row, :], NT, preferred_element_type=F32) * expo
             if back == 0:
-                k_tok = lax.broadcasted_iota(jnp.int32, (tok, TILE), 0)
+                k_tok = lax.broadcasted_iota(jnp.int32, s.shape, 0)
                 r_tok = (
-                    i * (TILE // per_group)
-                    + lax.broadcasted_iota(jnp.int32, (tok, TILE), 1) // per_group
+                    i * (TILE // per_group) + lax.broadcasted_iota(jnp.int32, s.shape, 1) // per_group
                 )
                 s = jnp.where(k_tok <= r_tok, s, FAR)
-            scores[rows, at_row] = s
+            scores[keys, at_row] = s
             tops[back : back + 1, at_row] = jnp.max(s, axis=0, keepdims=True)
-            dprob[rows, at_row] = lax.dot_general(
-                vals[rows, :], do_all[at_row, :], NT, preferred_element_type=F32
+            dprob[keys, at_row] = lax.dot_general(
+                vals[keys, :], do_all[at_row, :], NT, preferred_element_type=F32
             )
-            return carry
-
-        lax.fori_loop(0, tiles, step, 0, unroll=UNROLL)
 
     score_block(0)
     for group in groups[n_head - LAG :]:
@@ -339,39 +352,53 @@
             )
         score_block(slot)
 
-    def normalise(i, carry):
-        at_row = lanes_of(i)
+    for i in range(tiles):
+        at_row = pl.ds(i * TILE, TILE)
         top = jnp.max(tops[0:SPAN, at_row], axis=0, keepdims=True)
         mass = jnp.zeros_like(top)
         moment = jnp.zeros_like(top)
         for back in range(SPAN):
-            rows = rows_of(back)
-            e = jnp.exp2(scores[rows, at_row] - top)
-            scores[rows, at_row] = e
+            keys = needed(back, i)
+            e = jnp.exp2(scores[keys, at_row] - top)
+            scores[keys, at_row] = e
             mass = mass + jnp.sum(e, axis=0, keepdims=True)
-            moment = moment + jnp.sum(e * dprob[rows, at_row], axis=0, keepdims=True)
+            moment = moment + jnp.sum(e * dprob[keys, at_row], axis=0, keepdims=True)
         inverse = 1.0 / mass
         share[:, at_row] = inverse
         fix[:, at_row] = moment * inverse
-        return carry
-
-    lax.fori_loop(0, tiles, normalise, 0)
+
+    def weigh(keys, at_row):
+        p = scores[keys, at_row] * share[:, at_row]
+        low[keys, at_row] = p.astype(BF16)
+        dsc[keys, at_row] = (p * (dprob[keys, at_row] - fix[:, at_row])).astype(BF16)
 
     def gradient_block(back):
-        rows = rows_of(back)
-
-        def step(i, carry):
-            at_row = lanes_of(i)
-            p = scores[rows, at_row] * share[:, at_row]
-            low[rows, at_row] = p.astype(BF16)
-            dsc[rows, at_row] = (p * (dprob[rows, at_row] - fix[:, at_row])).astype(BF16)
-            return carry
-
-        lax.fori_loop(0, tiles, step, 0)
-        d_k = jnp.dot(dsc[rows, :], qx[:, pl.ds(0, head_dim)], preferred_element_type=F32) * inv_root
-        d_v = jnp.dot(low[rows, :], do_all[...], preferred_element_type=F32)
+        base, half = (BACK - back) * tok, tok // 2
+        if back in (0, BACK):
+            for i in range(tiles):
+                weigh(needed(back, i), pl.ds(i * TILE, TILE))
+            lower = pl.ds(0, n_rows) if back == 0 else pl.ds(0, n_rows // 2)
+            upper = pl.ds(n_rows // 2, n_rows // 2) if back == 0 else pl.ds(0, n_rows)
+            pieces = ((pl.ds(base, half), lower), (pl.ds(base + half, half), upper))
+        else:
+
+            def step(i, carry):
+                weigh(rows_of(back), lanes_of(i))
+                return carry
+
+            lax.fori_loop(0, tiles, step, 0)
+            pieces = ((rows_of(back), pl.ds(0, n_rows)),)
+        d_k = [
+            jnp.dot(dsc[keys, rows], qx[rows, pl.ds(0, head_dim)], preferred_element_type=F32)
+            for keys, rows in pieces
+        ]
+        d_v = [
+            jnp.dot(low[keys, rows], do_all[rows, :], preferred_element_type=F32)
+            for keys, rows in pieces
+        ]
         shape = (n_head, group_rows, head_dim)
-        return d_k.reshape(shape), d_v.reshape(shape)
+        d_k = jnp.concatenate(d_k, axis=0) * inv_root
+        return d_k.reshape(shape), jnp.concatenate(d_v, axis=0).reshape(shape)
 
     def settle(back):
         for which, term in enumerate(gradient_block(back)):
@@ -423,7 +450,7 @@
         o_ref[at_row, :] = out.T.astype(BF16)
         return carry
 
-    lax.fori_loop(0, tiles, attended, 0)
+    lax.fori_loop(0, tiles // 2, attended, 0, unroll=UNROLL)
     for off in home_order:
         group = lax.rem(head + off, n_head)
         awaited(
@@ -450,7 +477,8 @@
         dq_ref[at_row, :] = out.T.astype(BF16)
         return carry
 
-    lax.fori_loop(0, tiles, d_queries, 0)
+    lax.fori_loop(tiles // 2, tiles, attended, 0, unroll=UNROLL)
+    lax.fori_loop(0, tiles, d_queries, 0, unroll=UNROLL)
     for off in order:
         group = lax.rem(head + off, n_head)
         if off:

time: 44.6 us -> 42.7 us (0.957)
  Pallas kernels: 43.8 us -> 41.9 us
    pallas_call x1, Pallas kernels: 42.8 us -> 40.8 us  [on_device(): pl.pallas_call(functools.partial(fused_kernel, n_ctx, n_head), out_shape=...]
where the time goes in v3:
time: 42.7 us; the launch traced here: 42.5 us
  Pallas kernels  41.9 us (98%)
  between operations  0.64 us (1%)
    pallas_call x1, Pallas kernels, on_device(): pl.pallas_call(functools.partial(fused_kernel, n_ctx, n_head), out_shape=...  40.8 us
    pallas_call x1, Pallas kernels, on_device(): pl.pallas_call(store_kernel, out_shape=results, in_specs=[vmem] * 4, out_...  1.03 us

profile of v3, /device:TPU:1, one launch (start us, length us, event | category | flops | bytes accessed | tf_op | source)
XLA Modules:
  0.0 42.5 jit_solution(15432231002385692635)
XLA Ops:
  0.6 40.8 %shard_map.84 = (bf16[2048,128]{1,0:T(8,128)(2,1)S(1)}, bf16[2048,128]{1,0:T(8,128)(2,1)S(1)}, bf16[256,128]{1,0:T(8,128)(2,1)S(1)}, bf16[256,128]{1,0:T(8,128)(2,1)S(1)}) custom-call(bf16[2048,128]{1,0:T(8,128)(2,1)} %bitcast.9, bf16[256,128]{1,0:T(8,128)(2,1)} %bitcast.11, bf16[256,128]{1,0:T(8,128)(2,1)} %bitcast.12, bf16[2048,128]{1,0:T(8,128)(2,1)} %bitcast.10, ...), custom_call_target="tpu_custom_call" | custom-call | tf_op jit(solution)/shard_map/pallas_call | solution.py:524
  41.5 1.0 %shard_map.85 = (bf16[2048,128]{1,0:T(8,128)(2,1)}, bf16[2048,128]{1,0:T(8,128)(2,1)}, bf16[256,128]{1,0:T(8,128)(2,1)}, bf16[256,128]{1,0:T(8,128)(2,1)}) custom-call(bf16[2048,128]{1,0:T(8,128)(2,1)S(1)} %get-tuple-element.12.refs_0_, bf16[2048,128]{1,0:T(8,128)(2,1)S(1)} %get-tuple-element.13.refs_1_, bf16[256,128]{1,0:T(8,128)(2,1)S(1)} %get-tuple-element.14.refs_2_, ...), custom_call_target="tpu_custom_call" | custom-call | tf_op jit(solution)/shard_map/pallas_call | solution.py:576

commit v4 on v3

--- a/solution.py
+++ b/solution.py
@@ -309,6 +309,9 @@
     def lanes_of(i):
         return pl.ds(pl.multiple_of(i * TILE, TILE), TILE)
 
+    def in_pieces(keys):
+        return [pl.ds(keys.start + at_key, 32) for at_key in range(0, keys.size, 32)]
+
     def score_block(back):
         rows = rows_of(back)
         key_rows = span[back, :, 0].reshape(tok, head_dim)
@@ -355,14 +358,17 @@
     for i in range(tiles):
         at_row = pl.ds(i * TILE, TILE)
         top = jnp.max(tops[0:SPAN, at_row], axis=0, keepdims=True)
-        mass = jnp.zeros_like(top)
-        moment = jnp.zeros_like(top)
+        mass = jnp.zeros((8, TILE), F32)
+        moment = jnp.zeros((8, TILE), F32)
         for back in range(SPAN):
-            keys = needed(back, i)
-            e = jnp.exp2(scores[keys, at_row] - top)
-            scores[keys, at_row] = e
-            mass = mass + jnp.sum(e, axis=0, keepdims=True)
-            moment = moment + jnp.sum(e * dprob[keys, at_row], axis=0, keepdims=True)
+            for keys in in_pieces(needed(back, i)):
+                e = jnp.exp2(scores[keys, at_row] - top)
+                scores[keys, at_row] = e
+                mass = mass + jnp.sum(e.reshape(-1, 8, TILE), axis=0)
+                term = e * dprob[keys, at_row]
+                moment = moment + jnp.sum(term.reshape(-1, 8, TILE), axis=0)
+        mass = jnp.sum(mass, axis=0, keepdims=True)
+        moment = jnp.sum(moment, axis=0, keepdims=True)
         inverse = 1.0 / mass
         share[:, at_row] = inverse
         fix[:, at_row] = moment * inverse
@@ -376,7 +382,8 @@
         base, half = (BACK - back) * tok, tok // 2
         if back in (0, BACK):
             for i in range(tiles):
-                weigh(needed(back, i), pl.ds(i * TILE, TILE))
+                for keys in in_pieces(needed(back, i)):
+                    weigh(keys, pl.ds(i * TILE, TILE))
             lower = pl.ds(0, n_rows) if back == 0 else pl.ds(0, n_rows // 2)
             upper = pl.ds(n_rows // 2, n_rows // 2) if back == 0 else pl.ds(0, n_rows)
             pieces = ((pl.ds(base, half), lower), (pl.ds(base + half, half), upper))
@@ -408,6 +415,18 @@
     def _():
         pl.semaphore_wait(ready, 1)
 
+    home_order = order[::-1]
+
+    def piece(slot, off, to):
+        group = lax.rem(head + off, n_head)
+        return remote(
+            part.at[slot, group],
+            land.at[slot, group],
+            back_send.at[slot, off],
+            back_recv.at[slot, group],
+            {"ctx": to},
+        )
+
     far_there = back_two & on_one
     near_there = (core == 0) | back_two
     for back, slot, to, there in (
@@ -415,24 +434,14 @@
         (1, 0, partner, (core == 1) | back_two),
     ):
         settle(back)
-        started(
-            remote(
-                part.at[slot], land.at[slot], back_send.at[slot, 0], back_recv.at[slot, 0], {"ctx": to}
-            ),
-            there,
-        )
+        for off in home_order:
+            started(piece(slot, off, to), there)
     settle(2)
-    for slot, to, there in ((2, at(-1), far_there), (0, partner, near_there)):
-        awaited(
-            remote(
-                part.at[slot], land.at[slot], back_send.at[slot, 0], back_recv.at[slot, 0], {"ctx": to}
-            ),
-            there,
-        )
     on_second = (core == 1).astype(F32)
-    home_order = order[::-1]
     for off in home_order:
         group = lax.rem(head + off, n_head)
+        awaited(piece(2, off, at(-1)), far_there)
+        awaited(piece(0, off, partner), near_there)
         term = part[1, group].astype(F32) + land[2, group].astype(F32)
         second[group] = (term + on_second * land[0, group].astype(F32)).astype(BF16)
         started(

time: 42.7 us -> 42.7 us (level)
  no operation moved by 1% of the time
where the time goes in v4:
time: 42.7 us; the launch traced here: 42.5 us
  Pallas kernels  41.9 us (98%)
  between operations  0.64 us (1%)
    pallas_call x1, Pallas kernels, on_device(): pl.pallas_call(functools.partial(fused_kernel, n_ctx, n_head), out_shape=...  40.9 us
    pallas_call x1, Pallas kernels, on_device(): pl.pallas_call(store_kernel, out_shape=results, in_specs=[vmem] * 4, out_...  1.03 us

profile of v4, /device:TPU:1, one launch (start us, length us, event | category | flops | bytes accessed | tf_op | source)
XLA Modules:
  0.0 42.5 jit_solution(8844601888691119304)
XLA Ops:
  0.6 40.9 %shard_map.84 = (bf16[2048,128]{1,0:T(8,128)(2,1)S(1)}, bf16[2048,128]{1,0:T(8,128)(2,1)S(1)}, bf16[256,128]{1,0:T(8,128)(2,1)S(1)}, bf16[256,128]{1,0:T(8,128)(2,1)S(1)}) custom-call(bf16[2048,128]{1,0:T(8,128)(2,1)} %bitcast.9, bf16[256,128]{1,0:T(8,128)(2,1)} %bitcast.11, bf16[256,128]{1,0:T(8,128)(2,1)} %bitcast.12, bf16[2048,128]{1,0:T(8,128)(2,1)} %bitcast.10, ...), custom_call_target="tpu_custom_call" | custom-call | tf_op jit(solution)/shard_map/pallas_call | solution.py:533
  41.5 1.0 %shard_map.85 = (bf16[2048,128]{1,0:T(8,128)(2,1)}, bf16[2048,128]{1,0:T(8,128)(2,1)}, bf16[256,128]{1,0:T(8,128)(2,1)}, bf16[256,128]{1,0:T(8,128)(2,1)}) custom-call(bf16[2048,128]{1,0:T(8,128)(2,1)S(1)} %get-tuple-element.12.refs_0_, bf16[2048,128]{1,0:T(8,128)(2,1)S(1)} %get-tuple-element.13.refs_1_, bf16[256,128]{1,0:T(8,128)(2,1)S(1)} %get-tuple-element.14.refs_2_, ...), custom_call_target="tpu_custom_call" | custom-call | tf_op jit(solution)/shard_map/pallas_call | solution.py:585
